TPU v7x, 32 devices: a whole 2x2x4 slice. The times are simulated.
32 devices in a mesh: dp: 8 (over z, x), ctx: 4 (over y, core).
Axes of the slice: x: 2, y: 2, z: 4, core: 2. Of those that a mesh axis runs over, the one named last changes fastest.
Arguments:
- block_input: bfloat16 [8, 512, 1024], P('dp', 'ctx'), may hold values from -6 to 6
- segment_ids: int32 [8, 512], P('dp'), may hold values from 0 to 2, never falling along the last dimension, each value on 1 to 320 neighbouring positions
- ln1_gain: bfloat16 [1024], P('dp'), may hold values from 0.25 to 1.75
- ln1_bias: bfloat16 [1024], P('dp'), may hold values from -3 to 3
- qkv_weight: bfloat16 [1024, 3, 1024], P('dp', None, 'ctx'), may hold values from -3 to 3
- query_bias: bfloat16 [1024], P('dp'), may hold values from -3 to 3
- value_bias: bfloat16 [1024], P('dp'), may hold values from -1.1953125 to 1.1953125
- proj_weight: bfloat16 [1024, 1024], P('ctx', 'dp'), may hold values from -0.75 to 0.75
- proj_bias: bfloat16 [1024], P('dp'), may hold values from -3 to 3
- ln2_gain: bfloat16 [1024], P('dp'), may hold values from 0.25 to 1.75
- ln2_bias: bfloat16 [1024], P('dp'), may hold values from -3 to 3
- fc_weight: bfloat16 [1024, 4096], P('dp', 'ctx'), may hold values from -0.1875 to 0.1875
- fc_bias: bfloat16 [4096], P('dp'), may hold values from -3 to 3
- out_weight: bfloat16 [4096, 1024], P('ctx', 'dp'), may hold values from -0.09375 to 0.09375
- out_bias: bfloat16 [1024], P('dp'), may hold values from -3 to 3
- cotangent: bfloat16 [8, 512, 1024], P('dp', 'ctx'), may hold values from -6 to 6
Outputs:
- block_output: bfloat16 [8, 512, 1024], P('dp', 'ctx')
- input_grad: float32 [8, 512, 1024], P('dp', 'ctx')
- ln1_gain_grad: float32 [1024], P('dp')
- ln1_bias_grad: float32 [1024], P('dp')
- qkv_weight_grad: float32 [1024, 3, 1024], P('dp', None, 'ctx')
- query_bias_grad: float32 [1024], P('dp')
- value_bias_grad: float32 [1024], P('dp')
- proj_weight_grad: float32 [1024, 1024], P('ctx', 'dp')
- proj_bias_grad: float32 [1024], P('dp')
- ln2_gain_grad: float32 [1024], P('dp')
- ln2_bias_grad: float32 [1024], P('dp')
- fc_weight_grad: float32 [1024, 4096], P('dp', 'ctx')
- fc_bias_grad: float32 [4096], P('dp')
- out_weight_grad: float32 [4096, 1024], P('ctx', 'dp')
- out_bias_grad: float32 [1024], P('dp')
Inputs may be any that keep to these rules, and one draw needn't show every extreme that they name: `segment_ids`: segment numbers never fall along a sequence.
All inputs are finite; a program needn't handle non-finite values.
Results may differ from a plain program's by a relative error of at most 0.019.
Values may be sent and summed in bfloat16 or wider, within the bound.
A program may use at most 128 MiB of HBM per device.

v0:
```python
import jax
import jax.numpy as jnp
from jax import lax
from jax.sharding import PartitionSpec as P

D = 1024
HD = 64
FF = 4096


NORM_EPS = 1e-05
GELU_ROOT = 0.7978845608028654
GELU_CUBE = 0.044715
MASK_VALUE = -1e30


def norm_forward(residual):
    row_mean = jnp.mean(residual, axis=-1, keepdims=True)
    centered = residual - row_mean
    row_var = jnp.mean(centered * centered, axis=-1, keepdims=True)
    inv_std = lax.rsqrt(row_var + NORM_EPS)
    return (centered * inv_std, inv_std)


def norm_backward(grad_in, normed, inv_std, gain):
    scaled = grad_in * gain
    mean_scaled = jnp.mean(scaled, axis=-1, keepdims=True)
    mean_cross = jnp.mean(scaled * normed, axis=-1, keepdims=True)
    return inv_std * (scaled - mean_scaled - normed * mean_cross)


def gelu_pair(pre_act):
    inner_arg = GELU_ROOT * (pre_act + GELU_CUBE * pre_act * pre_act * pre_act)
    tangent = jnp.tanh(inner_arg)
    activated = 0.5 * pre_act * (1.0 + tangent)
    gelu_slope = 0.5 * (1.0 + tangent) + 0.5 * pre_act * (1.0 - tangent * tangent) * GELU_ROOT * (
        1.0 + 3.0 * GELU_CUBE * pre_act * pre_act
    )
    return (activated, gelu_slope)


def masked_scores(query_heads, key_heads, allowed):
    raw_scores = jnp.einsum(
        "qhd,khd->hqk", query_heads, key_heads, preferred_element_type=jnp.float32
    ) * HD ** (-0.5)
    return jnp.where(allowed[None], raw_scores, MASK_VALUE)


def attend(query_heads, key_heads, value_heads, allowed):
    scores = masked_scores(query_heads, key_heads, allowed)
    top_score = jnp.max(scores, axis=-1, keepdims=True)
    log_total = top_score + jnp.log(jnp.sum(jnp.exp(scores - top_score), axis=-1, keepdims=True))
    attn_probs = jnp.where(allowed[None], jnp.exp(scores - log_total), 0.0)
    probs_half = attn_probs.astype(jnp.bfloat16)
    attended = jnp.einsum(
        "hqk,khd->qhd", probs_half, value_heads, preferred_element_type=jnp.float32
    )
    return (attended.reshape(query_heads.shape[0], -1).astype(jnp.bfloat16), log_total)


def attend_back(query_heads, key_heads, value_heads, allowed, log_total, grad_heads):
    scores = masked_scores(query_heads, key_heads, allowed)
    attn_probs = jnp.where(allowed[None], jnp.exp(scores - log_total), 0.0)
    probs_half = attn_probs.astype(jnp.bfloat16)
    prob_grad = jnp.einsum(
        "qhd,khd->hqk", grad_heads, value_heads, preferred_element_type=jnp.float32
    )
    value_part = jnp.einsum(
        "hqk,qhd->khd", probs_half, grad_heads, preferred_element_type=jnp.float32
    )
    delta_rows = jnp.sum(attn_probs * prob_grad, axis=-1, keepdims=True)
    score_grad = (attn_probs * (prob_grad - delta_rows) * HD ** (-0.5)).astype(jnp.bfloat16)
    query_grad = jnp.einsum(
        "hqk,khd->qhd", score_grad, key_heads, preferred_element_type=jnp.float32
    )
    key_part = jnp.einsum(
        "hqk,qhd->khd", score_grad, query_heads, preferred_element_type=jnp.float32
    )
    key_count = key_heads.shape[0]
    return (
        query_grad.reshape(query_heads.shape[0], -1),
        key_part.reshape(key_count, -1),
        value_part.reshape(key_count, -1),
    )


def place_part(part, whole_len, start):
    return lax.dynamic_update_slice_in_dim(jnp.zeros((whole_len,), jnp.float32), part, start, 0)


def body(
    block_input,
    segment_ids,
    ln1_gain,
    ln1_bias,
    qkv_weight,
    query_bias,
    value_bias,
    proj_weight,
    proj_bias,
    ln2_gain,
    ln2_bias,
    fc_weight,
    fc_bias,
    out_weight,
    out_bias,
    cotangent,
):
    tokens = block_input[0]
    seg_whole = segment_ids[0]
    grad_rows = cotangent[0]
    seq_length = seg_whole.shape[0]
    ctx_rank = lax.axis_index("ctx")
    key_pos = jnp.arange(seq_length, dtype=jnp.int32)
    resid_in = tokens.astype(jnp.float32)
    normed_one, inv_one = norm_forward(resid_in)
    grad_out = grad_rows.astype(jnp.float32)
    out_shift_grad = jnp.sum(grad_out, axis=0)
    shards = (
        lax.all_gather(qkv_weight, "dp", axis=0, tiled=True),
        lax.all_gather(proj_weight, "dp", axis=1, tiled=True),
        lax.all_gather(fc_weight, "dp", axis=0, tiled=True),
        lax.all_gather(out_weight, "dp", axis=1, tiled=True),
        lax.all_gather(ln1_gain, "dp", axis=0, tiled=True),
        lax.all_gather(ln1_bias, "dp", axis=0, tiled=True),
        lax.all_gather(query_bias, "dp", axis=0, tiled=True),
        lax.all_gather(value_bias, "dp", axis=0, tiled=True),
        lax.all_gather(proj_bias, "dp", axis=0, tiled=True),
        lax.all_gather(ln2_gain, "dp", axis=0, tiled=True),
        lax.all_gather(ln2_bias, "dp", axis=0, tiled=True),
        lax.all_gather(fc_bias, "dp", axis=0, tiled=True),
        lax.all_gather(out_bias, "dp", axis=0, tiled=True),
    )
    qkv_cols = shards[0].reshape(D, -1)
    proj_rows = shards[1]
    fc_cols = shards[2]
    out_rows = shards[3]
    quarter = proj_rows.shape[0]
    unit_part = fc_cols.shape[1]
    gain_first = shards[4].astype(jnp.float32)
    shift_first = shards[5].astype(jnp.float32)
    query_shift = lax.dynamic_slice_in_dim(
        shards[6].astype(jnp.float32), ctx_rank * quarter, quarter
    )
    value_shift = lax.dynamic_slice_in_dim(
        shards[7].astype(jnp.float32), ctx_rank * quarter, quarter
    )
    proj_shift = shards[8].astype(jnp.float32)
    gain_second = shards[9].astype(jnp.float32)
    shift_second = shards[10].astype(jnp.float32)
    fc_shift = lax.dynamic_slice_in_dim(
        shards[11].astype(jnp.float32), ctx_rank * unit_part, unit_part
    )
    out_shift = shards[12].astype(jnp.float32)
    local_heads = quarter // HD
    allowed = (key_pos[:, None] >= key_pos[None, :]) & (seg_whole[:, None] == seg_whole[None, :])
    hidden_one = (normed_one * gain_first + shift_first).astype(jnp.bfloat16)
    hidden_all, grad_all = (
        lax.all_gather(hidden_one, "ctx", axis=0, tiled=True),
        lax.all_gather(grad_rows, "ctx", axis=0, tiled=True),
    )
    qkv_out = jnp.dot(hidden_all, qkv_cols, preferred_element_type=jnp.float32)
    queries = (qkv_out[:, :quarter] + query_shift).astype(jnp.bfloat16)
    keys_here = qkv_out[:, quarter : 2 * quarter].astype(jnp.bfloat16)
    values_here = (qkv_out[:, 2 * quarter :] + value_shift).astype(jnp.bfloat16)
    query_heads = queries.reshape(seq_length, local_heads, HD)
    key_heads = keys_here.reshape(seq_length, local_heads, HD)
    value_heads = values_here.reshape(seq_length, local_heads, HD)
    attended, log_total = attend(query_heads, key_heads, value_heads, allowed)
    resid_mid = (
        resid_in
        + lax.psum_scatter(
            jnp.dot(attended, proj_rows, preferred_element_type=jnp.float32).astype(jnp.bfloat16),
            "ctx",
            scatter_dimension=0,
            tiled=True,
        ).astype(jnp.float32)
        + proj_shift
    )
    normed_two, inv_two = norm_forward(resid_mid)
    hidden_two = (normed_two * gain_second + shift_second).astype(jnp.bfloat16)
    hidden_two_all = lax.all_gather(hidden_two, "ctx", axis=0, tiled=True)
    pre_act = jnp.dot(hidden_two_all, fc_cols, preferred_element_type=jnp.float32) + fc_shift
    activated, gelu_slope = gelu_pair(pre_act)
    activated = activated.astype(jnp.bfloat16)
    block_output = (
        resid_mid
        + lax.psum_scatter(
            jnp.dot(activated, out_rows, preferred_element_type=jnp.float32).astype(jnp.bfloat16),
            "ctx",
            scatter_dimension=0,
            tiled=True,
        ).astype(jnp.float32)
        + out_shift
    ).astype(jnp.bfloat16)
    out_weight_grad = jnp.dot(activated.T, grad_all, preferred_element_type=jnp.float32)
    pre_grad = jnp.dot(grad_all, out_rows.T, preferred_element_type=jnp.float32) * gelu_slope
    fc_shift_grad = place_part(jnp.sum(pre_grad, axis=0), FF, ctx_rank * unit_part)
    pre_grad_half = pre_grad.astype(jnp.bfloat16)
    fc_weight_grad = jnp.dot(hidden_two_all.T, pre_grad_half, preferred_element_type=jnp.float32)
    hidden_two_grad = lax.psum_scatter(
        jnp.dot(pre_grad_half, fc_cols.T, preferred_element_type=jnp.float32).astype(jnp.bfloat16),
        "ctx",
        scatter_dimension=0,
        tiled=True,
    ).astype(jnp.float32)
    gain_second_grad = jnp.sum(hidden_two_grad * normed_two, axis=0)
    shift_second_grad = jnp.sum(hidden_two_grad, axis=0)
    mid_grad = grad_out + norm_backward(hidden_two_grad, normed_two, inv_two, gain_second)
    proj_shift_grad = jnp.sum(mid_grad, axis=0)
    mid_grad_half = mid_grad.astype(jnp.bfloat16)
    mid_all = lax.all_gather(mid_grad_half, "ctx", axis=0, tiled=True)
    proj_weight_grad = jnp.dot(attended.T, mid_all, preferred_element_type=jnp.float32)
    attended_grad = jnp.dot(mid_all, proj_rows.T, preferred_element_type=jnp.float32).astype(
        jnp.bfloat16
    )
    grad_heads = attended_grad.reshape(seq_length, local_heads, HD)
    query_grad, key_grad, value_grad = attend_back(
        query_heads, key_heads, value_heads, allowed, log_total, grad_heads
    )
    query_shift_grad = place_part(jnp.sum(query_grad, axis=0), D, ctx_rank * quarter)
    value_shift_grad = place_part(jnp.sum(value_grad, axis=0), D, ctx_rank * quarter)
    qkv_grad = jnp.concatenate([query_grad, key_grad, value_grad], axis=1).astype(jnp.bfloat16)
    qkv_weight_grad = jnp.dot(hidden_all.T, qkv_grad, preferred_element_type=jnp.float32).reshape(
        D, 3, quarter
    )
    hidden_one_grad = lax.psum_scatter(
        jnp.dot(qkv_grad, qkv_cols.T, preferred_element_type=jnp.float32).astype(jnp.bfloat16),
        "ctx",
        scatter_dimension=0,
        tiled=True,
    ).astype(jnp.float32)
    gain_first_grad = jnp.sum(hidden_one_grad * normed_one, axis=0)
    shift_first_grad = jnp.sum(hidden_one_grad, axis=0)
    input_grad = mid_grad + norm_backward(hidden_one_grad, normed_one, inv_one, gain_first)
    finished = (
        lax.psum_scatter(qkv_weight_grad, "dp", scatter_dimension=0, tiled=True),
        lax.psum_scatter(proj_weight_grad, "dp", scatter_dimension=1, tiled=True),
        lax.psum_scatter(fc_weight_grad, "dp", scatter_dimension=0, tiled=True),
        lax.psum_scatter(out_weight_grad, "dp", scatter_dimension=1, tiled=True),
        lax.psum_scatter(gain_first_grad, "dp", scatter_dimension=0, tiled=True),
        lax.psum_scatter(shift_first_grad, "dp", scatter_dimension=0, tiled=True),
        lax.psum_scatter(query_shift_grad, "dp", scatter_dimension=0, tiled=True),
        lax.psum_scatter(value_shift_grad, "dp", scatter_dimension=0, tiled=True),
        lax.psum_scatter(proj_shift_grad, "dp", scatter_dimension=0, tiled=True),
        lax.psum_scatter(gain_second_grad, "dp", scatter_dimension=0, tiled=True),
        lax.psum_scatter(shift_second_grad, "dp", scatter_dimension=0, tiled=True),
        lax.psum_scatter(fc_shift_grad, "dp", scatter_dimension=0, tiled=True),
        lax.psum_scatter(out_shift_grad, "dp", scatter_dimension=0, tiled=True),
    )
    matrix_sums = finished[:4]
    vector_sums = lax.psum(
        (
            finished[4],
            finished[5],
            finished[6],
            finished[7],
            finished[8],
            finished[9],
            finished[10],
            finished[11],
            finished[12],
        ),
        "ctx",
    )
    return (
        block_output[None],
        input_grad[None],
        vector_sums[0],
        vector_sums[1],
        matrix_sums[0],
        vector_sums[2],
        vector_sums[3],
        matrix_sums[1],
        vector_sums[4],
        vector_sums[5],
        vector_sums[6],
        matrix_sums[2],
        vector_sums[7],
        matrix_sums[3],
        vector_sums[8],
    )


def solution(mesh):
    return jax.shard_map(
        body,
        mesh=mesh,
        in_specs=(
            P("dp", "ctx", None),
            P("dp", None),
            P("dp"),
            P("dp"),
            P("dp", None, "ctx"),
            P("dp"),
            P("dp"),
            P("ctx", "dp"),
            P("dp"),
            P("dp"),
            P("dp"),
            P("dp", "ctx"),
            P("dp"),
            P("ctx", "dp"),
            P("dp"),
            P("dp", "ctx", None),
        ),
        out_specs=(
            P("dp", "ctx", None),
            P("dp", "ctx", None),
            P("dp"),
            P("dp"),
            P("dp", None, "ctx"),
            P("dp"),
            P("dp"),
            P("ctx", "dp"),
            P("dp"),
            P("dp"),
            P("dp"),
            P("dp", "ctx"),
            P("dp"),
            P("ctx", "dp"),
            P("dp"),
        ),
        check_vma=False,
    )
```

profile of v0, /device:TPU:0, one launch (start us, length us, event | category | flops | bytes accessed | tf_op | source)
XLA Modules:
  0.0 759.7 jit_solution(2532319612262917514)
XLA Ops:
  8.3 1.2 fusion.49
  9.5 22.4 %all-gather.1 = bf16[8,1,128]{2,1,0:T(2,128)(2,1)S(1)} all-gather(bf16[1,1,128]{2,1,0:T(2,128)(2,1)} %bitcast.167), channel_id=1, replica_groups=mesh['dp'=8,'ctx'=4] {'dp'}, dimensions={0}, use_global_device_ids=true | all-gather | bytes 2304 | tf_op jit(solution)/shard_map/all_gather | solution.py:124
  31.9 16.5 %all-gather.2 = bf16[8,1,128]{2,1,0:T(2,128)(2,1)S(1)} all-gather(bf16[1,1,128]{2,1,0:T(2,128)(2,1)} %bitcast.168), channel_id=1, replica_groups=mesh['dp'=8,'ctx'=4] {'dp'}, dimensions={0}, use_global_device_ids=true | all-gather | bytes 2304 | tf_op jit(solution)/shard_map/all_gather | solution.py:125
  48.4 1.9 fusion.44
  50.4 1.7 copy.51
  52.2 18.3 %all-gather.4 = bf16[8,1,128]{2,1,0:T(2,128)(2,1)S(1)} all-gather(bf16[1,1,128]{2,1,0:T(2,128)(2,1)} %bitcast.169), channel_id=1, replica_groups=mesh['dp'=8,'ctx'=4] {'dp'}, dimensions={0}, use_global_device_ids=true | all-gather | bytes 2304 | tf_op jit(solution)/shard_map/all_gather | solution.py:126
  70.6 16.5 %all-gather.3 = bf16[8,1,128]{2,1,0:T(2,128)(2,1)S(1)} all-gather(bf16[1,1,128]{2,1,0:T(2,128)(2,1)} %bitcast.170), channel_id=1, replica_groups=mesh['dp'=8,'ctx'=4] {'dp'}, dimensions={0}, use_global_device_ids=true | all-gather | bytes 2304 | tf_op jit(solution)/shard_map/all_gather | solution.py:127
  87.2 29.2 %all_gather.57 = bf16[256,1024]{1,0:T(8,128)(2,1)S(1)} all-gather(bf16[256,128]{1,0:T(8,128)(2,1)} %param.23), channel_id=1, replica_groups=mesh['dp'=8,'ctx'=4] {'dp'}, dimensions={1}, use_global_device_ids=true | all-gather | bytes 589824 | tf_op jit(solution)/shard_map/all_gather | solution.py:121
  116.7 2.8 fusion.79
  123.0 1.3 convolution_convert_fusion.5
  124.3 1.5 convolution_convert_fusion.3
  126.5 18.9 %all-gather.5 = bf16[8,1,128]{2,1,0:T(2,128)(2,1)S(1)} all-gather(bf16[1,1,128]{2,1,0:T(2,128)(2,1)S(1)} %bitcast.171), channel_id=1, replica_groups=mesh['dp'=8,'ctx'=4] {'dp'}, dimensions={0}, use_global_device_ids=true | all-gather | bytes 2304 | tf_op jit(solution)/shard_map/all_gather | solution.py:128
  145.4 16.3 %all-gather.6 = bf16[8,1,128]{2,1,0:T(2,128)(2,1)S(1)} all-gather(bf16[1,1,128]{2,1,0:T(2,128)(2,1)S(1)} %bitcast.172), channel_id=1, replica_groups=mesh['dp'=8,'ctx'=4] {'dp'}, dimensions={0}, use_global_device_ids=true | all-gather | bytes 2304 | tf_op jit(solution)/shard_map/all_gather | solution.py:129
  161.7 18.3 %all-gather.7 = bf16[8,1,128]{2,1,0:T(2,128)(2,1)S(1)} all-gather(bf16[1,1,128]{2,1,0:T(2,128)(2,1)S(1)} %bitcast.173), channel_id=1, replica_groups=mesh['dp'=8,'ctx'=4] {'dp'}, dimensions={0}, use_global_device_ids=true | all-gather | bytes 2304 | tf_op jit(solution)/shard_map/all_gather | solution.py:130
  182.3 1.8 add_convert_fusion.1
  185.5 26.3 %all-gather.8 = bf16[8,1,512]{2,1,0:T(2,128)(2,1)S(1)} all-gather(bf16[1,1,512]{2,1,0:T(2,128)(2,1)S(1)} %reshape.192), channel_id=1, replica_groups=mesh['dp'=8,'ctx'=4] {'dp'}, dimensions={0}, use_global_device_ids=true | all-gather | bytes 9216 | tf_op jit(solution)/shard_map/all_gather | solution.py:131
  211.9 6.9 all-gather.22.cloned.1.call-done
  218.8 4.5 fusion.80
  223.3 13.7 %all-gather.30.cloned.1.call-done = bf16[1,512,1024]{2,1,0:T(8,128)(2,1)} async-done(((bf16[1,128,1024]{2,1,0:T(8,128)(2,1)}), bf16[1,512,1024]{2,1,0:T(8,128)(2,1)}) %all-gather.30.cloned.1.call-update) | async-done | bytes 1048592 | tf_op jit(solution)/shard_map/all_gather | solution.py:160
  237.0 52.4 %all-gather.26.cloned.1.call-done = bf16[1024,1024]{1,0:T(8,128)(2,1)} async-done(((bf16[1024,128]{1,0:T(8,128)(2,1)}), bf16[1024,1024]{1,0:T(8,128)(2,1)}) %all-gather.26.cloned.1.call-update) | async-done | bytes 2097168 | tf_op jit(solution)/shard_map/all_gather | solution.py:123
  289.4 5.1 fusion.78
  295.5 2.3 convolution_convert_fusion.1
  298.1 4.7 convolution_convert_fusion.2
  302.9 17.7 %all-gather.9 = bf16[8,1,128]{2,1,0:T(2,128)(2,1)S(1)} all-gather(bf16[1,1,128]{2,1,0:T(2,128)(2,1)S(1)} %bitcast.174), channel_id=1, replica_groups=mesh['dp'=8,'ctx'=4] {'dp'}, dimensions={0}, use_global_device_ids=true | all-gather | bytes 2304 | tf_op jit(solution)/shard_map/all_gather | solution.py:132
  321.0 1.3 fusion.56
  322.3 26.0 %reduce-scatter.11.cloned.1.call-done = bf16[128,1024]{1,0:T(8,128)(2,1)} async-done(((bf16[512,1024]{1,0:T(8,128)(2,1)}), bf16[128,1024]{1,0:T(8,128)(2,1)}) %reduce-scatter.11.cloned.1.call-update) | async-done | bytes 262160 | tf_op jit(solution)/shard_map/reduce_scatter | solution.py:188
  348.3 2.0 fusion.72
  352.0 16.8 %all-gather.28.cloned.1.call-done = bf16[512,1024]{1,0:T(8,128)(2,1)} async-done(((bf16[128,1024]{1,0:T(8,128)(2,1)}), bf16[512,1024]{1,0:T(8,128)(2,1)}) %all-gather.28.cloned.1.call-update) | async-done | bytes 1048592 | tf_op jit(solution)/shard_map/all_gather | solution.py:212
  368.8 1.7 convolution_convert_fusion.4
  370.5 3.7 fusion.74
  374.2 2.7 fusion.81
  376.9 7.5 fusion.22
  384.4 9.0 %fusion.75 = (f32[4,64]{1,0:T(4,128)S(1)}, bf16[512,4,64]{0,2,1:T(8,128)(2,1)S(1)}) fusion(bf16[512,4,64]{0,2,1:T(8,128)(2,1)S(1)} %bitcast.136, f32[4,512,512]{1,2,0:T(8,128)} %fusion.81, f32[4,512]{1,0:T(4,128)S(1)} %log_add_fusion, f32[4,512,512]{1,2,0:T(8,128)} %copy-done.1, pred[512,512]{0,1:T(8,128)(4,1)S(1)} %fusion.30), kind=kOutput, calls=%fused_computation.107 | convolution fusion | flops 148113664 | bytes 9184256 | tf_op jit(solution)/shard_map/hqk,khd->qhd/dot_general | solution.py:73
  393.4 3.6 convolution_convert_fusion
  397.1 1.4 fusion.82
  398.6 5.4 fusion.25
  405.6 3.3 fusion.60
  409.0 2.5 fusion.63
  411.5 2.4 copy.59
  417.3 4.7 reduce-scatter.15.cloned.1.call-done
  422.0 1.2 fusion.57
  423.2 38.1 %all-reduce.9 = (f32[1024]{0:T(1024)S(1)}, f32[1024]{0:T(1024)S(1)}, f32[1024]{0:T(1024)S(1)}, f32[1024]{0:T(1024)S(1)}, f32[1024]{0:T(1024)S(1)}, /*index=5*/f3...) all-reduce(f32[1024]{0:T(1024)S(1)} %get-tuple-element.17, ...), channel_id=7, replica_groups=mesh['dp'=8,'ctx'=4] {'dp'}, use_global_device_ids=true, to_apply=%region_16.17.clone | all-reduce | flops 12288 | bytes 98304
  462.0 6.5 all-reduce.10
  468.4 2.0 fusion.48
  470.4 20.2 %reduce-scatter.19.cloned.1.call-done = f32[256,128]{1,0:T(8,128)} async-done(((f32[256,1024]{1,0:T(8,128)}), f32[256,128]{1,0:T(8,128)}) %reduce-scatter.19.cloned.1.call-update) | async-done | bytes 131088 | tf_op jit(solution)/shard_map/reduce_scatter | solution.py:238
  490.6 92.0 %reduce-scatter.23.cloned.1.call-done = f32[1024,128]{1,0:T(8,128)} async-done(((f32[1024,1024]{1,0:T(8,128)}), f32[1024,128]{1,0:T(8,128)}) %reduce-scatter.23.cloned.1.call-update) | async-done | bytes 524304 | tf_op jit(solution)/shard_map/reduce_scatter | solution.py:240
  582.6 92.0 %reduce-scatter.21.cloned.1.call-done = f32[128,1024]{1,0:T(8,128)} async-done(((f32[1024,1024]{1,0:T(8,128)}), f32[128,1024]{1,0:T(8,128)}) %reduce-scatter.21.cloned.1.call-update) | async-done | bytes 524304 | tf_op jit(solution)/shard_map/reduce_scatter | solution.py:239
  674.6 78.5 %reduce-scatter.17.cloned.1.call-done = f32[128,3,256]{2,0,1:T(8,128)} async-done(((f32[1024,3,256]{2,0,1:T(8,128)}), f32[128,3,256]{2,0,1:T(8,128)}) %reduce-scatter.17.cloned.1.call-update) | async-done | bytes 393232 | tf_op jit(solution)/shard_map/reduce_scatter | solution.py:237
  (131 shorter events, 17.4 us)
Async XLA Ops:
  7.2 109.2 %copy-start.14 = (s32[1,512]{1,0:T(1,128)S(1)}, s32[1,512]{1,0:T(1,128)}, u32[]{:S(2)}) copy-start(s32[1,512]{1,0:T(1,128)} %param.17) | copy-start | bytes 6148
  7.2 109.5 %all-gather.18.cloned.1.call-start = ((), (), s32[]{:S(2)}) async-start(), calls=%async_computation.8 | async-start | bytes 1310720 | tf_op jit(solution)/shard_map/all_gather | solution.py:159
  50.4 66.3 %all-gather.20.cloned.1.call-start = ((), (), s32[]{:S(2)}) async-start(), calls=%async_computation.9 | async-start | bytes 1769472 | tf_op jit(solution)/shard_map/all_gather | solution.py:120
  52.2 127.8 %reduce-scatter.9.cloned.1.call-start = ((), (), s32[]{:S(2)}) async-start(), calls=%async_computation.10 | async-start | bytes 1310720 | tf_op jit(solution)/shard_map/reduce_scatter | solution.py:172
  121.0 2.0 copy-start.1
  124.3 2.2 copy-start.16
  124.3 21.1 %copy-start.17 = (bf16[128]{0:T(256)(128)(2,1)S(1)}, bf16[128]{0:T(256)(128)(2,1)}, u32[]{:S(2)}) copy-start(bf16[128]{0:T(256)(128)(2,1)} %param.25) | copy-start | bytes 772
  124.3 37.3 %copy-start.18 = (bf16[128]{0:T(256)(128)(2,1)S(1)}, bf16[128]{0:T(256)(128)(2,1)}, u32[]{:S(2)}) copy-start(bf16[128]{0:T(256)(128)(2,1)} %param.26) | copy-start | bytes 772
  124.3 55.6 %copy-start = (bf16[1,128,1024]{2,1,0:T(8,128)(2,1)S(1)}, bf16[1,128,1024]{2,1,0:T(8,128)(2,1)}, u32[]{:S(2)}) copy-start(bf16[1,128,1024]{2,1,0:T(8,128)(2,1)} %param.16) | copy-start | bytes 786436
  125.8 59.6 %copy-start.15 = (bf16[512]{0:T(512)(128)(2,1)S(1)}, bf16[512]{0:T(512)(128)(2,1)}, u32[]{:S(2)}) copy-start(bf16[512]{0:T(512)(128)(2,1)} %param.28) | copy-start | bytes 3076
  125.9 86.0 %all-gather.24.cloned.1.call-start = ((), (), s32[]{:S(2)}) async-start(), calls=%async_computation.12 | async-start | bytes 2359296 | tf_op jit(solution)/shard_map/all_gather | solution.py:122
  126.4 92.4 %all-gather.22.cloned.1.call-start = ((), (), s32[]{:S(2)}) async-start(), calls=%async_computation.11 | async-start | bytes 1310720 | tf_op jit(solution)/shard_map/all_gather | solution.py:182
  184.1 52.9 %all-gather.30.cloned.1.call-start = ((), (), s32[]{:S(2)}) async-start(), calls=%async_computation.22 | async-start | bytes 1310720 | tf_op jit(solution)/shard_map/all_gather | solution.py:160
  184.7 104.7 %all-gather.26.cloned.1.call-start = ((), (), s32[]{:S(2)}) async-start(), calls=%async_computation.13 | async-start | bytes 2359296 | tf_op jit(solution)/shard_map/all_gather | solution.py:123
  185.4 135.5 %reduce-scatter.13.cloned.1.call-start = ((), (), s32[]{:S(2)}) async-start(), calls=%async_computation.15 | async-start | bytes 1310720 | tf_op jit(solution)/shard_map/reduce_scatter | solution.py:201
  289.4 6.1 copy-start.20
  294.5 1.0 copy-start.9
  297.8 5.1 copy-start.19
  297.9 23.1 %copy-start.2 = (bf16[128,1024]{1,0:T(8,128)(2,1)S(1)}, bf16[128,1024]{1,0:T(8,128)(2,1)}, u32[]{:S(2)}) copy-start(bf16[128,1024]{1,0:T(8,128)(2,1)} %reduce-scatter.9.cloned.1.call-done) | copy-start | bytes 786436
  297.9 50.5 %copy-start.5 = (bf16[1,128,1024]{2,1,0:T(8,128)(2,1)S(1)}, bf16[1,128,1024]{2,1,0:T(8,128)(2,1)}, u32[]{:S(2)}) copy-start(bf16[1,128,1024]{2,1,0:T(8,128)(2,1)} %param.31) | copy-start | bytes 786436
  297.9 50.4 %reduce-scatter.11.cloned.1.call-start = ((), (), s32[]{:S(2)}) async-start(), calls=%async_computation.14 | async-start | bytes 1310720 | tf_op jit(solution)/shard_map/reduce_scatter | solution.py:188
  302.8 65.9 %all-gather.28.cloned.1.call-start = ((), (), s32[]{:S(2)}) async-start(), calls=%async_computation.16 | async-start | bytes 1310720 | tf_op jit(solution)/shard_map/all_gather | solution.py:212
  350.4 0.8 copy-start.3
  351.9 70.1 %reduce-scatter.15.cloned.1.call-start = ((), (), s32[]{:S(2)}) async-start(), calls=%async_computation.17 | async-start | bytes 1310720 | tf_op jit(solution)/shard_map/reduce_scatter | solution.py:227
  374.2 19.2 %copy-start.11 = (bf16[512,4,64]{0,2,1:T(8,128)(2,1)}, bf16[512,4,64]{0,2,1:T(8,128)(2,1)S(1)}, u32[]{:S(2)}) copy-start(bf16[512,4,64]{0,2,1:T(8,128)(2,1)S(1)} %get-tuple-element.47) | copy-start | bytes 786436
  384.4 9.0 %copy-start.12 = (bf16[4,64,512]{2,1,0:T(8,128)(2,1)}, bf16[4,64,512]{2,1,0:T(8,128)(2,1)S(1)}, u32[]{:S(2)}) copy-start(bf16[4,64,512]{2,1,0:T(8,128)(2,1)S(1)} %fusion.22) | copy-start | bytes 786436
  393.4 3.6 copy-start.13
  393.4 3.7 copy-start.8
  397.0 93.6 %reduce-scatter.19.cloned.1.call-start = ((), (), s32[]{:S(2)}) async-start(), calls=%async_computation.19 | async-start | bytes 1179648 | tf_op jit(solution)/shard_map/reduce_scatter | solution.py:238
  398.5 184.1 %reduce-scatter.23.cloned.1.call-start = ((), (), s32[]{:S(2)}) async-start(), calls=%async_computation.21 | async-start | bytes 4718592 | tf_op jit(solution)/shard_map/reduce_scatter | solution.py:240
  404.0 1.3 copy-start.7
  404.0 1.6 copy-start.10
  404.0 270.6 %reduce-scatter.21.cloned.1.call-start = ((), (), s32[]{:S(2)}) async-start(), calls=%async_computation.20 | async-start | bytes 4718592 | tf_op jit(solution)/shard_map/reduce_scatter | solution.py:239
  408.9 344.2 %reduce-scatter.17.cloned.1.call-start = ((), (), s32[]{:S(2)}) async-start(), calls=%async_computation.18 | async-start | bytes 3538944 | tf_op jit(solution)/shard_map/reduce_scatter | solution.py:237
  413.8 0.7 copy-start.21
  413.8 2.5 copy-start.6
  413.8 54.6 %copy-start.4 = (f32[128,1024]{1,0:T(8,128)S(1)}, f32[128,1024]{1,0:T(8,128)}, u32[]{:S(2)}) copy-start(f32[128,1024]{1,0:T(8,128)} %copy-done.3) | copy-start | bytes 1572868
Sparse Core Ops, SparseCore 0:
  50.5 15.3 all-gather.17
  68.5 47.4 all-gather.19
  126.0 24.0 reduce-scatter.8
  152.1 49.4 all-gather.23
  203.5 15.2 all-gather.21
  220.2 16.6 all-gather.29
  239.0 50.3 all-gather.25
  298.0 22.9 reduce-scatter.12
  323.5 24.7 reduce-scatter.10
  352.1 16.6 all-gather.27
  397.2 24.7 reduce-scatter.14
  425.8 64.7 reduce-scatter.18
  494.8 87.7 reduce-scatter.22
  586.7 87.9 reduce-scatter.20
  678.7 74.4 reduce-scatter.16
where the time goes:
time: 760 us
  waiting for transfers between devices  406 us (53%)
  blocking collectives  245 us (32%)
  matrix products  63.8 us (8%)
  other arithmetic  16.9 us (2%)
  between operations  15.6 us (2%)
  local copies, waits for them, and re-layouts  11.8 us (2%)
    reduce_scatter x1, waiting for transfers between devices, body(): lax.psum_scatter(fc_weight_grad, 'dp', scatter_dimension=0, tiled=True)  92 us
    reduce_scatter x1, waiting for transfers between devices, body(): lax.psum_scatter(out_weight_grad, 'dp', scatter_dimension=1, tiled=True)  92 us
    reduce_scatter x1, waiting for transfers between devices, body(): lax.psum_scatter(qkv_weight_grad, 'dp', scatter_dimension=0, tiled=True)  78.5 us
    all_gather x1, waiting for transfers between devices, body(): lax.all_gather(out_weight, 'dp', axis=1, tiled=True)  52.4 us
    unnamed x1, blocking collectives  38.1 us
    all_gather x1, blocking collectives, body(): lax.all_gather(proj_weight, 'dp', axis=1, tiled=True)  29.2 us
    all_gather x1, blocking collectives, body(): lax.all_gather(fc_bias, 'dp', axis=0, tiled=True)  26.3 us
    reduce_scatter x1, waiting for transfers between devices, body(): lax.psum_scatter(jnp.dot(activated, out_rows, preferred_element_type=jnp....  26 us
  transfers between devices with their start and end apart: 15, of which 11 were waited for; matrix products, arithmetic and copies ran while one was open for 5% of the time, Pallas kernels for 0%

commit v1 on v0

--- a/solution.py
+++ b/solution.py
@@ -116,42 +116,37 @@
     normed_one, inv_one = norm_forward(resid_in)
     grad_out = grad_rows.astype(jnp.float32)
     out_shift_grad = jnp.sum(grad_out, axis=0)
-    shards = (
-        lax.all_gather(qkv_weight, "dp", axis=0, tiled=True),
-        lax.all_gather(proj_weight, "dp", axis=1, tiled=True),
-        lax.all_gather(fc_weight, "dp", axis=0, tiled=True),
-        lax.all_gather(out_weight, "dp", axis=1, tiled=True),
-        lax.all_gather(ln1_gain, "dp", axis=0, tiled=True),
-        lax.all_gather(ln1_bias, "dp", axis=0, tiled=True),
-        lax.all_gather(query_bias, "dp", axis=0, tiled=True),
-        lax.all_gather(value_bias, "dp", axis=0, tiled=True),
-        lax.all_gather(proj_bias, "dp", axis=0, tiled=True),
-        lax.all_gather(ln2_gain, "dp", axis=0, tiled=True),
-        lax.all_gather(ln2_bias, "dp", axis=0, tiled=True),
-        lax.all_gather(fc_bias, "dp", axis=0, tiled=True),
-        lax.all_gather(out_bias, "dp", axis=0, tiled=True),
-    )
-    qkv_cols = shards[0].reshape(D, -1)
-    proj_rows = shards[1]
-    fc_cols = shards[2]
-    out_rows = shards[3]
+    vectors = lax.all_gather(
+        jnp.concatenate(
+            [ln1_gain, ln1_bias, query_bias, value_bias, proj_bias, ln2_gain, ln2_bias, out_bias, fc_bias]
+        ),
+        "dp",
+        axis=0,
+    )
+    slice_len = ln1_gain.shape[0]
+    dp_size = vectors.shape[0]
+    ff_whole = fc_bias.shape[0] * dp_size
+
+    def vector(at):
+        return vectors[:, at * slice_len : (at + 1) * slice_len].astype(jnp.float32).reshape(-1)
+
+    qkv_cols = lax.all_gather(qkv_weight, "dp", axis=0, tiled=True).reshape(D, -1)
+    proj_rows = lax.all_gather(proj_weight, "dp", axis=1, tiled=True)
+    fc_cols = lax.all_gather(fc_weight, "dp", axis=0, tiled=True)
+    out_rows = lax.all_gather(out_weight, "dp", axis=1, tiled=True)
     quarter = proj_rows.shape[0]
     unit_part = fc_cols.shape[1]
-    gain_first = shards[4].astype(jnp.float32)
-    shift_first = shards[5].astype(jnp.float32)
-    query_shift = lax.dynamic_slice_in_dim(
-        shards[6].astype(jnp.float32), ctx_rank * quarter, quarter
-    )
-    value_shift = lax.dynamic_slice_in_dim(
-        shards[7].astype(jnp.float32), ctx_rank * quarter, quarter
-    )
-    proj_shift = shards[8].astype(jnp.float32)
-    gain_second = shards[9].astype(jnp.float32)
-    shift_second = shards[10].astype(jnp.float32)
+    gain_first = vector(0)
+    shift_first = vector(1)
+    query_shift = lax.dynamic_slice_in_dim(vector(2), ctx_rank * quarter, quarter)
+    value_shift = lax.dynamic_slice_in_dim(vector(3), ctx_rank * quarter, quarter)
+    proj_shift = vector(4)
+    gain_second = vector(5)
+    shift_second = vector(6)
+    out_shift = vector(7)
     fc_shift = lax.dynamic_slice_in_dim(
-        shards[11].astype(jnp.float32), ctx_rank * unit_part, unit_part
-    )
-    out_shift = shards[12].astype(jnp.float32)
+        vectors[:, 8 * slice_len :].astype(jnp.float32).reshape(-1), ctx_rank * unit_part, unit_part
+    )
     local_heads = quarter // HD
     allowed = (key_pos[:, None] >= key_pos[None, :]) & (seg_whole[:, None] == seg_whole[None, :])
     hidden_one = (normed_one * gain_first + shift_first).astype(jnp.bfloat16)
@@ -195,7 +190,7 @@
     ).astype(jnp.bfloat16)
     out_weight_grad = jnp.dot(activated.T, grad_all, preferred_element_type=jnp.float32)
     pre_grad = jnp.dot(grad_all, out_rows.T, preferred_element_type=jnp.float32) * gelu_slope
-    fc_shift_grad = place_part(jnp.sum(pre_grad, axis=0), FF, ctx_rank * unit_part)
+    fc_shift_grad = place_part(jnp.sum(pre_grad, axis=0), ff_whole, ctx_rank * unit_part)
     pre_grad_half = pre_grad.astype(jnp.bfloat16)
     fc_weight_grad = jnp.dot(hidden_two_all.T, pre_grad_half, preferred_element_type=jnp.float32)
     hidden_two_grad = lax.psum_scatter(
@@ -233,36 +228,36 @@
     gain_first_grad = jnp.sum(hidden_one_grad * normed_one, axis=0)
     shift_first_grad = jnp.sum(hidden_one_grad, axis=0)
     input_grad = mid_grad + norm_backward(hidden_one_grad, normed_one, inv_one, gain_first)
-    finished = (
-        lax.psum_scatter(qkv_weight_grad, "dp", scatter_dimension=0, tiled=True),
-        lax.psum_scatter(proj_weight_grad, "dp", scatter_dimension=1, tiled=True),
-        lax.psum_scatter(fc_weight_grad, "dp", scatter_dimension=0, tiled=True),
-        lax.psum_scatter(out_weight_grad, "dp", scatter_dimension=1, tiled=True),
-        lax.psum_scatter(gain_first_grad, "dp", scatter_dimension=0, tiled=True),
-        lax.psum_scatter(shift_first_grad, "dp", scatter_dimension=0, tiled=True),
-        lax.psum_scatter(query_shift_grad, "dp", scatter_dimension=0, tiled=True),
-        lax.psum_scatter(value_shift_grad, "dp", scatter_dimension=0, tiled=True),
-        lax.psum_scatter(proj_shift_grad, "dp", scatter_dimension=0, tiled=True),
-        lax.psum_scatter(gain_second_grad, "dp", scatter_dimension=0, tiled=True),
-        lax.psum_scatter(shift_second_grad, "dp", scatter_dimension=0, tiled=True),
-        lax.psum_scatter(fc_shift_grad, "dp", scatter_dimension=0, tiled=True),
-        lax.psum_scatter(out_shift_grad, "dp", scatter_dimension=0, tiled=True),
-    )
-    matrix_sums = finished[:4]
-    vector_sums = lax.psum(
-        (
-            finished[4],
-            finished[5],
-            finished[6],
-            finished[7],
-            finished[8],
-            finished[9],
-            finished[10],
-            finished[11],
-            finished[12],
-        ),
-        "ctx",
-    )
+    half = jnp.bfloat16
+    matrix_sums = (
+        lax.psum_scatter(qkv_weight_grad.astype(half), "dp", scatter_dimension=0, tiled=True),
+        lax.psum_scatter(proj_weight_grad.astype(half), "dp", scatter_dimension=1, tiled=True),
+        lax.psum_scatter(fc_weight_grad.astype(half), "dp", scatter_dimension=0, tiled=True),
+        lax.psum_scatter(out_weight_grad.astype(half), "dp", scatter_dimension=1, tiled=True),
+    )
+    matrix_sums = tuple(m.astype(jnp.float32) for m in matrix_sums)
+    packed = jnp.concatenate(
+        [
+            v.reshape(dp_size, -1)
+            for v in (
+                gain_first_grad,
+                shift_first_grad,
+                query_shift_grad,
+                value_shift_grad,
+                proj_shift_grad,
+                gain_second_grad,
+                shift_second_grad,
+                out_shift_grad,
+                fc_shift_grad,
+            )
+        ],
+        axis=1,
+    )
+    packed = lax.psum(packed, ("dp", "ctx"))
+    mine = lax.dynamic_index_in_dim(packed, lax.axis_index("dp"), 0, keepdims=False)
+    order = (0, 1, 2, 3, 4, 5, 6, 8, 7)
+    pieces = [mine[i * slice_len : (i + 1) * slice_len] for i in range(8)] + [mine[8 * slice_len :]]
+    vector_sums = tuple(pieces[i] for i in order)
     return (
         block_output[None],
         input_grad[None],

time: 760 us -> 679 us (0.89)
  blocking collectives: 245 us -> 99.8 us
  waiting for transfers between devices: 406 us -> 456 us
  local copies, waits for them, and re-layouts: 11.8 us -> 21.7 us
    reduce_scatter x4 -> x2, waiting for transfers between devices: 283 us -> 93.9 us  [the longest x1 68.9 us: body(): lax.psum_scatter(fc_weight_grad.astype(half), 'dp', scatter_dimension=0,...]
    all_gather x10 -> x2, blocking collectives: 200 us -> 59.6 us  [the longest x1 32.6 us: body(): lax.all_gather(jnp.concatenate([ln1_gain, ln1_bias, query_bias, value_bia...]
    unnamed x15 -> x17, waiting for transfers between devices: 1.94 us -> 103 us
    all_gather x3, waiting for transfers between devices: 52.5 us -> 133 us  [the longest x1 52.4 us: body(): out_rows = lax.all_gather(out_weight, 'dp', axis=1, tiled=True)]
    unnamed x1 -> x0, blocking collectives: 38.1 us -> none
    psum x1, blocking collectives: 6.46 us -> 40.2 us  [body(): packed = lax.psum(packed, ('dp', 'ctx'))]
    reduce_scatter x1, waiting for transfers between devices: 0.01 us -> 22.5 us  [body(): lax.psum_scatter(jnp.dot(attended, proj_rows, preferred_element_type=jnp....]
    reduce_scatter x1, waiting for transfers between devices: 4.69 us -> 24.6 us  [body(): lax.psum_scatter(jnp.dot(qkv_grad, qkv_cols.T, preferred_element_type=jnp...]
  transfers between devices with their start and end apart: 15 -> 15, of which waited for: 11 -> 14; matrix products, arithmetic and copies ran while one was open for 5% -> 11% of each run, Pallas kernels for 0% -> 0%
where the time goes in v1:
time: 679 us; the launch traced here: 678 us
  waiting for transfers between devices  456 us (67%)
  blocking collectives  99.8 us (15%)
  matrix products  63.1 us (9%)
  other arithmetic  21.9 us (3%)
  local copies, waits for them, and re-layouts  21.7 us (3%)
  between operations  14.3 us (2%)
    unnamed x17, waiting for transfers between devices  103 us
    reduce_scatter x1, waiting for transfers between devices, body(): lax.psum_scatter(fc_weight_grad.astype(half), 'dp', scatter_dimension=0,...  68.9 us
    all_gather x1, waiting for transfers between devices, body(): out_rows = lax.all_gather(out_weight, 'dp', axis=1, tiled=True)  52.4 us
    all_gather x1, waiting for transfers between devices, body(): fc_cols = lax.all_gather(fc_weight, 'dp', axis=0, tiled=True)  45.4 us
    psum x1, blocking collectives, body(): packed = lax.psum(packed, ('dp', 'ctx'))  40.2 us
    all_gather x1, waiting for transfers between devices, body(): lax.all_gather(qkv_weight, 'dp', axis=0, tiled=True).reshape(D, -1)  35.4 us
    all_gather x1, blocking collectives, body(): lax.all_gather(jnp.concatenate([ln1_gain, ln1_bias, query_bias, value_bia...  32.6 us
    all_gather x1, blocking collectives, body(): proj_rows = lax.all_gather(proj_weight, 'dp', axis=1, tiled=True)  27 us
  transfers between devices with their start and end apart: 15, of which 14 were waited for; matrix products, arithmetic and copies ran while one was open for 11% of the time, Pallas kernels for 0%

profile of v1, /device:TPU:0, one launch (start us, length us, event | category | flops | bytes accessed | tf_op | source)
XLA Modules:
  0.0 677.9 jit_solution(5925180839455593192)
XLA Ops:
  8.3 1.2 fusion.48
  16.9 32.6 %all-gather.2 = bf16[8,1,1536]{2,1,0:T(2,128)(2,1)S(1)} all-gather(bf16[1,1,1536]{2,1,0:T(2,128)(2,1)S(1)} %reshape.258), channel_id=2, replica_groups=mesh['dp'=8,'ctx'=4] {'dp'}, dimensions={0}, use_global_device_ids=true | all-gather | bytes 27648 | tf_op jit(solution)/shard_map/all_gather | solution.py:119
  49.5 1.9 fusion.43
  51.5 1.7 copy.51
  53.4 27.0 %all_gather.34 = bf16[256,1024]{1,0:T(8,128)(2,1)S(1)} all-gather(bf16[256,128]{1,0:T(8,128)(2,1)S(1)} %copy-done.4), channel_id=1, replica_groups=mesh['dp'=8,'ctx'=4] {'dp'}, dimensions={1}, use_global_device_ids=true | all-gather | bytes 589824 | tf_op jit(solution)/shard_map/all_gather | solution.py:134
  80.7 35.4 %all-gather.13.cloned.1.call-done = bf16[1024,3,256]{0,2,1:T(8,128)(2,1)} async-done(((bf16[128,3,256]{0,2,1:T(8,128)(2,1)}), bf16[1024,3,256]{0,2,1:T(8,128)(2,1)}) %all-gather.13.cloned.1.call-update) | async-done | bytes 1572880 | tf_op jit(solution)/shard_map/all_gather | solution.py:133
  116.2 2.7 fusion.84
  122.4 1.3 convolution_convert_fusion.9
  123.7 1.4 convolution_convert_fusion.6
  125.8 22.5 %reduce-scatter.13.cloned.1.call-done = bf16[128,1024]{1,0:T(8,128)(2,1)} async-done(((bf16[512,1024]{1,0:T(8,128)(2,1)}), bf16[128,1024]{1,0:T(8,128)(2,1)}) %reduce-scatter.13.cloned.1.call-update) | async-done | bytes 262160 | tf_op jit(solution)/shard_map/reduce_scatter | solution.py:167
  148.3 1.1 fusion.62
  149.5 1.2 multiply_reduce_fusion.1
  150.6 1.8 add_convert_fusion.1
  154.1 45.4 %all-gather.17.cloned.1.call-done = bf16[1024,1024]{1,0:T(8,128)(2,1)} async-done(((bf16[128,1024]{1,0:T(8,128)(2,1)}), bf16[1024,1024]{1,0:T(8,128)(2,1)}) %all-gather.17.cloned.1.call-update) | async-done | bytes 2097168 | tf_op jit(solution)/shard_map/all_gather | solution.py:135
  199.4 17.2 %all-gather.15.cloned.1.call-done = bf16[512,1024]{1,0:T(8,128)(2,1)} async-done(((bf16[128,1024]{1,0:T(8,128)(2,1)}), bf16[512,1024]{1,0:T(8,128)(2,1)}) %all-gather.15.cloned.1.call-update) | async-done | bytes 1048592 | tf_op jit(solution)/shard_map/all_gather | solution.py:177
  216.7 4.5 fusion.85
  221.2 13.7 %all-gather.23.cloned.1.call-done = bf16[1,512,1024]{2,1,0:T(8,128)(2,1)} async-done(((bf16[1,128,1024]{2,1,0:T(8,128)(2,1)}), bf16[1,512,1024]{2,1,0:T(8,128)(2,1)}) %all-gather.23.cloned.1.call-update) | async-done | bytes 1048592 | tf_op jit(solution)/shard_map/all_gather | solution.py:155
  234.8 52.4 %all-gather.19.cloned.1.call-done = bf16[1024,1024]{1,0:T(8,128)(2,1)} async-done(((bf16[1024,128]{1,0:T(8,128)(2,1)}), bf16[1024,1024]{1,0:T(8,128)(2,1)}) %all-gather.19.cloned.1.call-update) | async-done | bytes 2097168 | tf_op jit(solution)/shard_map/all_gather | solution.py:136
  287.2 5.1 fusion.83
  292.3 2.3 convolution_convert_fusion.4
  294.8 4.8 convolution_convert_fusion.5
  299.6 18.2 %reduce-scatter.17.cloned.1.call-done = bf16[128,1024]{1,0:T(8,128)(2,1)} async-done(((bf16[512,1024]{1,0:T(8,128)(2,1)}), bf16[128,1024]{1,0:T(8,128)(2,1)}) %reduce-scatter.17.cloned.1.call-update) | async-done | bytes 262160 | tf_op jit(solution)/shard_map/reduce_scatter | solution.py:196
  317.8 1.3 fusion.55
  319.1 26.0 %reduce-scatter.15.cloned.1.call-done = bf16[128,1024]{1,0:T(8,128)(2,1)} async-done(((bf16[512,1024]{1,0:T(8,128)(2,1)}), bf16[128,1024]{1,0:T(8,128)(2,1)}) %reduce-scatter.15.cloned.1.call-update) | async-done | bytes 262160 | tf_op jit(solution)/shard_map/reduce_scatter | solution.py:183
  345.2 2.0 fusion.77
  348.0 4.8 convolution_convert_fusion
  352.9 4.0 copy.66
  357.0 4.2 convolution_convert_fusion.1
  361.2 3.6 all-gather.21.cloned.1.call-done
  364.9 1.7 convolution_convert_fusion.7
  367.5 1.7 convolution_convert_fusion.8
  369.2 2.7 fusion.86
  372.2 7.7 %fusion.22 = bf16[4,64,512]{2,1,0:T(8,128)(2,1)S(1)} fusion(bf16[512,4,64]{0,2,1:T(8,128)(2,1)S(1)} %bitcast.205, f32[4,512,512]{1,2,0:T(8,128)} %fusion.86, f32[4,512,512]{1,2,0:T(8,128)} %copy-done.1, f32[4,512]{1,0:T(4,128)S(1)} %log_add_fusion, pred[512,512]{0,1:T(8,128)(4,1)S(1)} %fusion.29), kind=kOutput, calls=%fused_computation.31 | convolution fusion | flops 147982848 | bytes 9183232 | tf_op jit(solution)/shard_map/hqk,qhd->khd/dot_general | solution.py:76
  379.9 9.0 %fusion.80 = (f32[4,64]{1,0:T(4,128)S(1)}, bf16[512,4,64]{0,2,1:T(8,128)(2,1)S(1)}) fusion(bf16[512,4,64]{0,2,1:T(8,128)(2,1)S(1)} %bitcast.203, f32[4,512,512]{1,2,0:T(8,128)} %fusion.86, f32[4,512]{1,0:T(4,128)S(1)} %log_add_fusion, f32[4,512,512]{1,2,0:T(8,128)} %copy-done.1, pred[512,512]{0,1:T(8,128)(4,1)S(1)} %fusion.29), kind=kOutput, calls=%fused_computation.144 | convolution fusion | flops 148113664 | bytes 9184256 | tf_op jit(solution)/shard_map/hqk,khd->qhd/dot_general | solution.py:73
  389.0 3.9 fusion.79
  392.9 2.0 convolution_convert_fusion.3
  395.0 2.4 convolution_convert_fusion.2
  397.3 1.6 copy.59
  399.9 37.2 %reduce-scatter.27.cloned.1.call-done = bf16[128,1024]{1,0:T(8,128)(2,1)} async-done(((bf16[1024,1024]{1,0:T(8,128)(2,1)}), bf16[128,1024]{1,0:T(8,128)(2,1)}) %reduce-scatter.27.cloned.1.call-update) | async-done | bytes 262160
  439.1 68.9 %reduce-scatter.23.cloned.1.call-done = bf16[128,1024]{1,0:T(8,128)(2,1)} async-done(((bf16[1024,1024]{1,0:T(8,128)(2,1)}), bf16[128,1024]{1,0:T(8,128)(2,1)}) %reduce-scatter.23.cloned.1.call-update) | async-done | bytes 262160 | tf_op jit(solution)/shard_map/reduce_scatter | solution.py:235
  508.0 1.8 convert_element_type.145
  509.8 63.9 %reduce-scatter.25.cloned.1.call-done = bf16[128,256]{1,0:T(8,128)(2,1)} async-done(((bf16[1024,256]{1,0:T(8,128)(2,1)}), bf16[128,256]{1,0:T(8,128)(2,1)}) %reduce-scatter.25.cloned.1.call-update) | async-done | bytes 65552
  575.3 24.6 %reduce-scatter.19.cloned.1.call-done = bf16[128,1024]{1,0:T(8,128)(2,1)} async-done(((bf16[512,1024]{1,0:T(8,128)(2,1)}), bf16[128,1024]{1,0:T(8,128)(2,1)}) %reduce-scatter.19.cloned.1.call-update) | async-done | bytes 262160 | tf_op jit(solution)/shard_map/reduce_scatter | solution.py:222
  599.8 1.2 fusion.56
  601.2 40.2 %psum.7 = f32[8,1536]{1,0:T(8,128)S(1)} all-reduce(f32[8,1536]{1,0:T(8,128)S(1)} %constant_dynamic-update-slice_fusion), channel_id=1, replica_groups=mesh['dp'=8,'ctx'=4] {'dp','ctx'}, use_global_device_ids=true, to_apply=%region_24.25 | all-reduce | flops 12288 | bytes 98304 | tf_op jit(solution)/shard_map/psum | solution.py:256
  642.7 2.0 fusion.47
  644.7 25.0 %reduce-scatter.21.cloned.1.call-done = bf16[128,3,256]{2,0,1:T(8,128)(2,1)} async-done(((bf16[1024,3,256]{2,0,1:T(8,128)(2,1)}), bf16[128,3,256]{2,0,1:T(8,128)(2,1)}) %reduce-scatter.21.cloned.1.call-update) | async-done | bytes 196624 | tf_op jit(solution)/shard_map/reduce_scatter | solution.py:233
  669.6 1.7 convert_element_type.141
  (115 shorter events, 22.9 us)
Async XLA Ops:
  7.2 46.3 %copy-start.4 = (bf16[256,128]{1,0:T(8,128)(2,1)S(1)}, bf16[256,128]{1,0:T(8,128)(2,1)}, u32[]{:S(2)}) copy-start(bf16[256,128]{1,0:T(8,128)(2,1)} %param.23) | copy-start | bytes 196612
  7.2 73.3 %copy-start.5 = (s32[1,512]{1,0:T(1,128)S(1)}, s32[1,512]{1,0:T(1,128)}, u32[]{:S(2)}) copy-start(s32[1,512]{1,0:T(1,128)} %param.17) | copy-start | bytes 6148
  7.2 73.5 %all-gather.11.cloned.1.call-start = ((), (), s32[]{:S(2)}) async-start(), calls=%async_computation.8 | async-start | bytes 1310720 | tf_op jit(solution)/shard_map/all_gather | solution.py:154
  51.4 64.8 %all-gather.13.cloned.1.call-start = ((), (), s32[]{:S(2)}) async-start(), calls=%async_computation.9 | async-start | bytes 1769472 | tf_op jit(solution)/shard_map/all_gather | solution.py:133
  53.2 95.1 %reduce-scatter.13.cloned.1.call-start = ((), (), s32[]{:S(2)}) async-start(), calls=%async_computation.10 | async-start | bytes 1310720 | tf_op jit(solution)/shard_map/reduce_scatter | solution.py:167
  120.4 2.0 copy-start.1
  123.7 24.6 %copy-start = (bf16[1,128,1024]{2,1,0:T(8,128)(2,1)S(1)}, bf16[1,128,1024]{2,1,0:T(8,128)(2,1)}, u32[]{:S(2)}) copy-start(bf16[1,128,1024]{2,1,0:T(8,128)(2,1)} %param.16) | copy-start | bytes 786436
  125.2 74.2 %all-gather.17.cloned.1.call-start = ((), (), s32[]{:S(2)}) async-start(), calls=%async_computation.12 | async-start | bytes 2359296 | tf_op jit(solution)/shard_map/all_gather | solution.py:135
  125.8 90.9 %all-gather.15.cloned.1.call-start = ((), (), s32[]{:S(2)}) async-start(), calls=%async_computation.11 | async-start | bytes 1310720 | tf_op jit(solution)/shard_map/all_gather | solution.py:177
  152.5 82.4 %all-gather.23.cloned.1.call-start = ((), (), s32[]{:S(2)}) async-start(), calls=%async_computation.20 | async-start | bytes 1310720 | tf_op jit(solution)/shard_map/all_gather | solution.py:155
  153.0 134.2 %all-gather.19.cloned.1.call-start = ((), (), s32[]{:S(2)}) async-start(), calls=%async_computation.13 | async-start | bytes 2359296 | tf_op jit(solution)/shard_map/all_gather | solution.py:136
  153.8 164.0 %reduce-scatter.17.cloned.1.call-start = ((), (), s32[]{:S(2)}) async-start(), calls=%async_computation.15 | async-start | bytes 1310720 | tf_op jit(solution)/shard_map/reduce_scatter | solution.py:196
  287.2 5.1 copy-start.6
  292.3 2.4 copy-start.10
  294.7 23.1 %copy-start.2 = (bf16[128,1024]{1,0:T(8,128)(2,1)S(1)}, bf16[128,1024]{1,0:T(8,128)(2,1)}, u32[]{:S(2)}) copy-start(bf16[128,1024]{1,0:T(8,128)(2,1)} %reduce-scatter.13.cloned.1.call-done) | copy-start | bytes 786436
  294.7 50.5 %copy-start.3 = (bf16[1,128,1024]{2,1,0:T(8,128)(2,1)S(1)}, bf16[1,128,1024]{2,1,0:T(8,128)(2,1)}, u32[]{:S(2)}) copy-start(bf16[1,128,1024]{2,1,0:T(8,128)(2,1)} %param.31) | copy-start | bytes 786436
  294.7 50.5 %reduce-scatter.15.cloned.1.call-start = ((), (), s32[]{:S(2)}) async-start(), calls=%async_computation.14 | async-start | bytes 1310720 | tf_op jit(solution)/shard_map/reduce_scatter | solution.py:183
  299.6 65.3 %all-gather.21.cloned.1.call-start = ((), (), s32[]{:S(2)}) async-start(), calls=%async_computation.16 | async-start | bytes 1310720 | tf_op jit(solution)/shard_map/all_gather | solution.py:207
  348.0 89.1 %reduce-scatter.27.cloned.1.call-start = ((), (), s32[]{:S(2)}) async-start(), calls=%async_computation.22 | async-start | bytes 2359296
  356.9 151.1 %reduce-scatter.23.cloned.1.call-start = ((), (), s32[]{:S(2)}) async-start(), calls=%async_computation.19 | async-start | bytes 2359296 | tf_op jit(solution)/shard_map/reduce_scatter | solution.py:235
  361.2 212.5 %reduce-scatter.25.cloned.1.call-start = ((), (), s32[]{:S(2)}) async-start(), calls=%async_computation.21 | async-start | bytes 589824
  371.9 227.9 %reduce-scatter.19.cloned.1.call-start = ((), (), s32[]{:S(2)}) async-start(), calls=%async_computation.17 | async-start | bytes 1310720 | tf_op jit(solution)/shard_map/reduce_scatter | solution.py:222
  388.9 3.9 copy-start.8
  389.0 3.9 copy-start.7
  392.9 2.0 copy-start.9
  394.9 274.7 %reduce-scatter.21.cloned.1.call-start = ((), (), s32[]{:S(2)}) async-start(), calls=%async_computation.18 | async-start | bytes 1769472 | tf_op jit(solution)/shard_map/reduce_scatter | solution.py:233
Sparse Core Ops, SparseCore 0:
  51.5 17.5 all-gather.10
  71.7 44.3 all-gather.12
  125.3 22.9 reduce-scatter.12
  150.3 49.0 all-gather.16
  201.4 15.2 all-gather.14
  218.1 16.6 all-gather.22
  236.9 50.3 all-gather.18
  294.8 22.9 reduce-scatter.16
  320.4 24.7 reduce-scatter.14
  348.1 16.6 all-gather.20
  368.4 68.6 reduce-scatter.26
  440.5 67.4 reduce-scatter.22
  511.9 61.6 reduce-scatter.24
  576.0 23.7 reduce-scatter.18
  603.1 66.4 reduce-scatter.20
